TPU v7x, 128 devices: a whole 4x4x4 slice. The times are simulated.
128 devices in a mesh: grp: 4 (over y), own: 32 (over x, z, core).
Axes of the slice: x: 4, y: 4, z: 4, core: 2. Of those that a mesh axis runs over, the one named last changes fastest.
Arguments:
- embeddings: float32 [98304, 768], P(('grp', 'own')), may hold values from -64 to 64
- cluster_ids: int32 [98304], P(('grp', 'own')), may hold values from 0 to 511, as said below
- owner_map: int32 [512], replicated, may hold values from 0 to 31, as said below
- source_order: int32 [98304], P(('grp', 'own')), may hold values from 0 to 767, as said below
Outputs:
- dup_score: float32 [98304], P(('grp', 'own'))
- centroids: float32 [512, 768], P('own')
Inputs may be any that keep to these rules, and one draw needn't show every extreme that they name: `owner_map`: every owner index is given to exactly 16 clusters. `cluster_ids`: within the 768 rows of one device, at most 48 rows have clusters of one owner index; in every draw some owner index receives exactly 48 rows from every device, and every device sends exactly 48 rows to some owner index. Cluster sizes are uneven and some clusters may be empty. `source_order`: each aligned block of 768 entries is a permutation of 0 to 767.
All inputs are finite; a program needn't handle non-finite values.
Results may differ from a plain program's by a relative error of at most 0.0003.
Values sent between devices are 32-bit elements; how exact they have to be, the bound alone decides.
A program may use at most 128 MiB of HBM per device.

v0:
```python
import jax
import jax.numpy as jnp
from jax import lax
from jax.sharding import PartitionSpec as P

CL_OWN = 16
sharpness = 6.0


def unit_rows(embeddings):
    squares = jnp.sum(embeddings * embeddings, axis=1, keepdims=True)
    return embeddings * lax.rsqrt(squares + 1e-06)


def owner_positions(owner_map):
    cluster_index = jnp.arange(owner_map.shape[0], dtype=jnp.int32)
    same_owner = owner_map[:, None] == owner_map[None, :]
    earlier = cluster_index[None, :] < cluster_index[:, None]
    before = jnp.sum((same_owner & earlier).astype(jnp.int32), axis=1)
    return owner_map * CL_OWN + before


def masked_weights(left_rows, left_ids, right_rows, right_ids):
    scores = jnp.einsum(
        "id,jd->ij",
        left_rows,
        right_rows,
        preferred_element_type=jnp.float32,
        precision=lax.Precision.HIGHEST,
    )
    linked = (left_ids[:, None] == right_ids[None, :]) & (left_ids[:, None] >= 0)
    return jnp.where(linked, jnp.exp(sharpness * (scores - 1.0)), 0.0)


def tile_sums(left_rows, left_ids, right_rows, right_ids):
    right_count = right_rows.shape[0]
    block_rows = 512
    block_count = right_count // block_rows
    right_blocks = right_rows.reshape(block_count, block_rows, right_rows.shape[1])
    id_blocks = right_ids.reshape(block_count, block_rows)

    def one_block(row_total, block_pair):
        weights = masked_weights(left_rows, left_ids, block_pair[0], block_pair[1])
        column_part = None
        return (row_total + jnp.sum(weights, axis=1), column_part)

    row_sums, column_sums = lax.scan(
        one_block, jnp.zeros((left_rows.shape[0],), jnp.float32), (right_blocks, id_blocks)
    )
    return (row_sums, column_sums)


def local(embeddings, cluster_ids, owner_map, source_order):
    row_count, feature_width = embeddings.shape
    owner_count = lax.axis_size("own")
    capacity = 2 * row_count // owner_count
    slot_count = owner_count * capacity
    cluster_count = owner_map.shape[0]
    unit_embed = unit_rows(embeddings)
    cluster_index = jnp.arange(cluster_count, dtype=jnp.int32)
    cluster_match = cluster_ids[:, None] == cluster_index[None, :]
    row_owner = jnp.sum(jnp.where(cluster_match, owner_map[None, :], 0), axis=1)
    owner_hot = (row_owner[:, None] == jnp.arange(owner_count, dtype=jnp.int32)[None, :]).astype(
        jnp.int32
    )
    rank_index = jnp.sum(jnp.cumsum(owner_hot, axis=0) * owner_hot, axis=1) - 1
    slot_index = row_owner * capacity + rank_index
    send_rows = jnp.zeros((slot_count, feature_width), jnp.float32).at[slot_index].set(unit_embed)
    send_ids = jnp.full((slot_count,), -1, jnp.int32).at[slot_index].set(cluster_ids)
    held_rows, held_ids = (
        lax.all_to_all(
            send_rows.reshape(owner_count, capacity, feature_width),
            "own",
            split_axis=0,
            concat_axis=0,
            tiled=True,
        ),
        lax.all_to_all(
            send_ids.reshape(owner_count, capacity), "own", split_axis=0, concat_axis=0, tiled=True
        ),
    )
    held_rows = held_rows.reshape(slot_count, feature_width)
    held_ids = held_ids.reshape(slot_count)
    row_sums, column_sums = tile_sums(
        held_rows,
        held_ids,
        lax.all_gather(held_rows, "grp", axis=0, tiled=True),
        lax.all_gather(held_ids, "grp", axis=0, tiled=True),
    )
    returned = lax.all_to_all(
        row_sums.reshape(owner_count, capacity), "own", split_axis=0, concat_axis=0, tiled=True
    )
    row_score = jnp.log(returned.reshape(slot_count)[slot_index])
    dup_score = jnp.zeros((row_count,), jnp.float32).at[source_order].set(row_score)
    position = owner_positions(owner_map)
    position_index = jnp.arange(cluster_count, dtype=jnp.int32)
    ordered = jnp.sum(
        jnp.where(position[None, :] == position_index[:, None], cluster_index[None, :], 0), axis=1
    )
    cluster_hot = (cluster_ids[:, None] == ordered[None, :]).astype(jnp.float32)
    cluster_terms = lax.dot_general(
        cluster_hot,
        unit_embed,
        (((0,), (0,)), ((), ())),
        preferred_element_type=jnp.float32,
        precision=lax.Precision.HIGHEST,
    )
    partial_value = lax.psum_scatter(cluster_terms, "own", scatter_dimension=0, tiled=True)
    cluster_sums = lax.psum(partial_value, "grp")
    centroids = cluster_sums * lax.rsqrt(
        jnp.mean(cluster_sums * cluster_sums, axis=1, keepdims=True) + 1e-06
    )
    return (dup_score, centroids)


def solution(mesh):
    placed = (P(("grp", "own"), None), P(("grp", "own")), P(), P(("grp", "own")))
    return jax.shard_map(
        local,
        mesh=mesh,
        in_specs=placed,
        out_specs=(P(("grp", "own")), P("own", None)),
        check_vma=False,
    )
```

profile of v0, /device:TPU:1, one launch (start us, length us, event | category | flops | bytes accessed | tf_op | source)
XLA Modules:
  0.0 433.6 jit_solution(5770465693371880921)
XLA Ops:
  8.0 1.2 select_reduce_fusion
  9.2 1.7 reduce-window.6
  11.0 0.3 slice_reduce_fusion
  11.3 0.1 fusion.22
  11.4 1.9 multiply_reduce_fusion
  13.3 9.7 %scatter_custom_fusion.1 = f32[1536,768]{1,0:T(8,128)} fusion(s32[768]{0:T(1024)S(1)} %fusion.26, f32[]{:T(128)} %constant.55.clone.1, f32[768,768]{1,0:T(8,128)S(1)} %copy-done, f32[768]{0:T(1024)S(1)} %add_rsqrt_fusion), kind=kCustom, calls=%fused_computation.17 | custom fusion | flops 589824 | bytes 7081988 | tf_op jit(solution)/shard_map/scatter | solution.py:68
  23.1 9.6 %all-to-all-start.1 = ((f32[32,48,768]{2,1,0:T(8,128)}), f32[32,48,768]{2,1,0:T(8,128)}, u32[]{:S(2)}, u32[]{:S(2)}) async-start(f32[32,48,768]{2,1,0:T(8,128)} %bitcast.46), calls=%async_computation.1 | async-start | bytes 9437184 | tf_op jit(solution)/shard_map/all_to_all | solution.py:71
  32.7 0.0 reduce-scatter.2.cloned.1.call-start
  32.8 0.2 convert_reduce_fusion
  33.0 0.2 select_reduce_fusion.1
  33.2 3.8 fusion.12
  37.0 0.0 all-gather.3.cloned.1.call-start
  37.1 55.2 %all-to-all-done.1 = f32[32,48,768]{2,1,0:T(8,128)} async-done(((f32[32,48,768]{2,1,0:T(8,128)}), f32[32,48,768]{2,1,0:T(8,128)}, u32[]{:S(2)}, u32[]{:S(2)}) %all-to-all-start.1) | async-done | bytes 4718624 | tf_op jit(solution)/shard_map/all_to_all | solution.py:71
  92.3 3.4 scatter_custom_fusion
  95.7 0.7 all_to_all.17
  96.4 9.8 %all-to-all-start = ((s32[32,1,48]{2,1,0:T(1,128)}), s32[32,1,48]{2,1,0:T(1,128)S(1)}, u32[]{:S(2)}, u32[]{:S(2)}) async-start(s32[32,1,48]{2,1,0:T(1,128)} %all_to_all.17), calls=%async_computation | async-start | bytes 32768 | tf_op jit(solution)/shard_map/all_to_all | solution.py:78
  106.2 6.8 %all-to-all-done = s32[32,1,48]{2,1,0:T(1,128)S(1)} async-done(((s32[32,1,48]{2,1,0:T(1,128)}), s32[32,1,48]{2,1,0:T(1,128)S(1)}, u32[]{:S(2)}, u32[]{:S(2)}) %all-to-all-start) | async-done | bytes 6176 | tf_op jit(solution)/shard_map/all_to_all | solution.py:78
  113.1 0.1 eq.172
  113.1 0.5 broadcast.158
  113.7 0.6 reduce.11
  114.3 0.1 reshape.149
  114.4 10.7 %all-gather = s32[4,1,1536]{2,1,0:T(1,128)S(1)} all-gather(s32[1,1,1536]{2,1,0:T(1,128)S(1)} %reshape.149), channel_id=1, replica_groups=mesh['grp'=4,'own'=32] {'grp'}, dimensions={0}, use_global_device_ids=true | all-gather | bytes 30720 | tf_op jit(solution)/shard_map/all_gather | solution.py:88
  125.0 0.1 reduce.3
  125.1 16.3 %psum.7 = f32[16,768]{1,0:T(8,128)S(1)} all-reduce(f32[16,768]{1,0:T(8,128)} %reduce-scatter.2.cloned.1.call-done), channel_id=1, replica_groups=mesh['grp'=4,'own'=32] {'grp'}, use_global_device_ids=true, to_apply=%region_14.15 | all-reduce | flops 12288 | bytes 98304 | tf_op jit(solution)/shard_map/psum | solution.py:109
  141.4 0.1 multiply_reduce_fusion.1
  141.6 127.8 %all-gather.3.cloned.1.call-done = f32[6144,768]{1,0:T(8,128)} async-done(((f32[1536,768]{1,0:T(8,128)}), f32[6144,768]{1,0:T(8,128)}) %all-gather.3.cloned.1.call-update) | async-done | bytes 18874384 | tf_op jit(solution)/shard_map/all_gather | solution.py:87
  269.4 131.6 %while.14 = (s32[]{:T(128)}, f32[1536]{0:T(1024)S(1)}, s32[32,48]{1,0:T(8,128)}, s32[12,512]{1,0:T(8,128)S(1)}, f32[12,512,768]{2,1,0:T(8,128)}, /*index=5*/f32[...) while((s32[]{:T(128)}, f32[1536]{0:T(1024)S(1)}, s32[32,48]{1,0:T(8,128)}, ...), condition=%wide.wide.region_9.10_spmd.clone, body=%wide.wide.region_7.9_spmd.clone.sunk | while | flops 7252478976 | bytes 6338155 | solution.py:47
  269.4 10.9 %fusion.38 = f32[1536]{0:T(1024)S(1)} fusion(f32[1536,768]{1,0:T(8,128)} %get-tuple-element.203, f32[12,512,768]{2,1,0:T(8,128)} %get-tuple-element.202, s32[]{:T(128)} %get-tuple-element.189, pred[1536]{0:T(1024)(128)(4,1)S(1)} %broadcast_compare_fusion.3, s32[512]{0:T(512)S(1)} %bitcast.50, s32[1536]{0:T(1024)S(1)} %get-tuple-element.204), kind=kOutput, calls=%fused_computation.11.clone.clone.1 | convolution fusion | flops 7252474368 | bytes 6307840 | tf_op jit(solution)/shard_map/while/body/eval_jaxpr/id,jd->ij/dot_general | solution.py:24
  280.4 10.9 %fusion.38 = f32[1536]{0:T(1024)S(1)} fusion(f32[1536,768]{1,0:T(8,128)} %get-tuple-element.203, f32[12,512,768]{2,1,0:T(8,128)} %get-tuple-element.202, s32[]{:T(128)} %get-tuple-element.189, pred[1536]{0:T(1024)(128)(4,1)S(1)} %broadcast_compare_fusion.3, s32[512]{0:T(512)S(1)} %bitcast.50, s32[1536]{0:T(1024)S(1)} %get-tuple-element.204), kind=kOutput, calls=%fused_computation.11.clone.clone.1 | convolution fusion | flops 7252474368 | bytes 6307840 | tf_op jit(solution)/shard_map/while/body/eval_jaxpr/id,jd->ij/dot_general | solution.py:24
  291.4 10.9 %fusion.38 = f32[1536]{0:T(1024)S(1)} fusion(f32[1536,768]{1,0:T(8,128)} %get-tuple-element.203, f32[12,512,768]{2,1,0:T(8,128)} %get-tuple-element.202, s32[]{:T(128)} %get-tuple-element.189, pred[1536]{0:T(1024)(128)(4,1)S(1)} %broadcast_compare_fusion.3, s32[512]{0:T(512)S(1)} %bitcast.50, s32[1536]{0:T(1024)S(1)} %get-tuple-element.204), kind=kOutput, calls=%fused_computation.11.clone.clone.1 | convolution fusion | flops 7252474368 | bytes 6307840 | tf_op jit(solution)/shard_map/while/body/eval_jaxpr/id,jd->ij/dot_general | solution.py:24
  302.3 10.9 %fusion.38 = f32[1536]{0:T(1024)S(1)} fusion(f32[1536,768]{1,0:T(8,128)} %get-tuple-element.203, f32[12,512,768]{2,1,0:T(8,128)} %get-tuple-element.202, s32[]{:T(128)} %get-tuple-element.189, pred[1536]{0:T(1024)(128)(4,1)S(1)} %broadcast_compare_fusion.3, s32[512]{0:T(512)S(1)} %bitcast.50, s32[1536]{0:T(1024)S(1)} %get-tuple-element.204), kind=kOutput, calls=%fused_computation.11.clone.clone.1 | convolution fusion | flops 7252474368 | bytes 6307840 | tf_op jit(solution)/shard_map/while/body/eval_jaxpr/id,jd->ij/dot_general | solution.py:24
  313.3 10.9 %fusion.38 = f32[1536]{0:T(1024)S(1)} fusion(f32[1536,768]{1,0:T(8,128)} %get-tuple-element.203, f32[12,512,768]{2,1,0:T(8,128)} %get-tuple-element.202, s32[]{:T(128)} %get-tuple-element.189, pred[1536]{0:T(1024)(128)(4,1)S(1)} %broadcast_compare_fusion.3, s32[512]{0:T(512)S(1)} %bitcast.50, s32[1536]{0:T(1024)S(1)} %get-tuple-element.204), kind=kOutput, calls=%fused_computation.11.clone.clone.1 | convolution fusion | flops 7252474368 | bytes 6307840 | tf_op jit(solution)/shard_map/while/body/eval_jaxpr/id,jd->ij/dot_general | solution.py:24
  324.3 10.9 %fusion.38 = f32[1536]{0:T(1024)S(1)} fusion(f32[1536,768]{1,0:T(8,128)} %get-tuple-element.203, f32[12,512,768]{2,1,0:T(8,128)} %get-tuple-element.202, s32[]{:T(128)} %get-tuple-element.189, pred[1536]{0:T(1024)(128)(4,1)S(1)} %broadcast_compare_fusion.3, s32[512]{0:T(512)S(1)} %bitcast.50, s32[1536]{0:T(1024)S(1)} %get-tuple-element.204), kind=kOutput, calls=%fused_computation.11.clone.clone.1 | convolution fusion | flops 7252474368 | bytes 6307840 | tf_op jit(solution)/shard_map/while/body/eval_jaxpr/id,jd->ij/dot_general | solution.py:24
  335.3 10.9 %fusion.38 = f32[1536]{0:T(1024)S(1)} fusion(f32[1536,768]{1,0:T(8,128)} %get-tuple-element.203, f32[12,512,768]{2,1,0:T(8,128)} %get-tuple-element.202, s32[]{:T(128)} %get-tuple-element.189, pred[1536]{0:T(1024)(128)(4,1)S(1)} %broadcast_compare_fusion.3, s32[512]{0:T(512)S(1)} %bitcast.50, s32[1536]{0:T(1024)S(1)} %get-tuple-element.204), kind=kOutput, calls=%fused_computation.11.clone.clone.1 | convolution fusion | flops 7252474368 | bytes 6307840 | tf_op jit(solution)/shard_map/while/body/eval_jaxpr/id,jd->ij/dot_general | solution.py:24
  346.2 10.9 %fusion.38 = f32[1536]{0:T(1024)S(1)} fusion(f32[1536,768]{1,0:T(8,128)} %get-tuple-element.203, f32[12,512,768]{2,1,0:T(8,128)} %get-tuple-element.202, s32[]{:T(128)} %get-tuple-element.189, pred[1536]{0:T(1024)(128)(4,1)S(1)} %broadcast_compare_fusion.3, s32[512]{0:T(512)S(1)} %bitcast.50, s32[1536]{0:T(1024)S(1)} %get-tuple-element.204), kind=kOutput, calls=%fused_computation.11.clone.clone.1 | convolution fusion | flops 7252474368 | bytes 6307840 | tf_op jit(solution)/shard_map/while/body/eval_jaxpr/id,jd->ij/dot_general | solution.py:24
  357.2 10.9 %fusion.38 = f32[1536]{0:T(1024)S(1)} fusion(f32[1536,768]{1,0:T(8,128)} %get-tuple-element.203, f32[12,512,768]{2,1,0:T(8,128)} %get-tuple-element.202, s32[]{:T(128)} %get-tuple-element.189, pred[1536]{0:T(1024)(128)(4,1)S(1)} %broadcast_compare_fusion.3, s32[512]{0:T(512)S(1)} %bitcast.50, s32[1536]{0:T(1024)S(1)} %get-tuple-element.204), kind=kOutput, calls=%fused_computation.11.clone.clone.1 | convolution fusion | flops 7252474368 | bytes 6307840 | tf_op jit(solution)/shard_map/while/body/eval_jaxpr/id,jd->ij/dot_general | solution.py:24
  368.2 10.9 %fusion.38 = f32[1536]{0:T(1024)S(1)} fusion(f32[1536,768]{1,0:T(8,128)} %get-tuple-element.203, f32[12,512,768]{2,1,0:T(8,128)} %get-tuple-element.202, s32[]{:T(128)} %get-tuple-element.189, pred[1536]{0:T(1024)(128)(4,1)S(1)} %broadcast_compare_fusion.3, s32[512]{0:T(512)S(1)} %bitcast.50, s32[1536]{0:T(1024)S(1)} %get-tuple-element.204), kind=kOutput, calls=%fused_computation.11.clone.clone.1 | convolution fusion | flops 7252474368 | bytes 6307840 | tf_op jit(solution)/shard_map/while/body/eval_jaxpr/id,jd->ij/dot_general | solution.py:24
  379.1 10.9 %fusion.38 = f32[1536]{0:T(1024)S(1)} fusion(f32[1536,768]{1,0:T(8,128)} %get-tuple-element.203, f32[12,512,768]{2,1,0:T(8,128)} %get-tuple-element.202, s32[]{:T(128)} %get-tuple-element.189, pred[1536]{0:T(1024)(128)(4,1)S(1)} %broadcast_compare_fusion.3, s32[512]{0:T(512)S(1)} %bitcast.50, s32[1536]{0:T(1024)S(1)} %get-tuple-element.204), kind=kOutput, calls=%fused_computation.11.clone.clone.1 | convolution fusion | flops 7252474368 | bytes 6307840 | tf_op jit(solution)/shard_map/while/body/eval_jaxpr/id,jd->ij/dot_general | solution.py:24
  390.1 10.9 %fusion.38 = f32[1536]{0:T(1024)S(1)} fusion(f32[1536,768]{1,0:T(8,128)} %get-tuple-element.203, f32[12,512,768]{2,1,0:T(8,128)} %get-tuple-element.202, s32[]{:T(128)} %get-tuple-element.189, pred[1536]{0:T(1024)(128)(4,1)S(1)} %broadcast_compare_fusion.3, s32[512]{0:T(512)S(1)} %bitcast.50, s32[1536]{0:T(1024)S(1)} %get-tuple-element.204), kind=kOutput, calls=%fused_computation.11.clone.clone.1 | convolution fusion | flops 7252474368 | bytes 6307840 | tf_op jit(solution)/shard_map/while/body/eval_jaxpr/id,jd->ij/dot_general | solution.py:24
  401.0 0.7 all_to_all.21
  401.7 7.7 %all-to-all-start.2 = ((f32[32,1,48]{2,1,0:T(1,128)}), f32[32,1,48]{2,1,0:T(1,128)S(1)}, u32[]{:S(2)}, u32[]{:S(2)}) async-start(f32[32,1,48]{2,1,0:T(1,128)} %all_to_all.21), calls=%async_computation.2 | async-start | bytes 32768 | tf_op jit(solution)/shard_map/all_to_all | solution.py:90
  409.5 0.7 broadcast_multiply_fusion
  410.2 6.2 %all-to-all-done.2 = f32[32,1,48]{2,1,0:T(1,128)S(1)} async-done(((f32[32,1,48]{2,1,0:T(1,128)}), f32[32,1,48]{2,1,0:T(1,128)S(1)}, u32[]{:S(2)}, u32[]{:S(2)}) %all-to-all-start.2) | async-done | bytes 6176 | tf_op jit(solution)/shard_map/all_to_all | solution.py:90
  416.4 0.5 broadcast.159
  416.9 0.7 reduce.12
  417.6 0.1 reshape.115
  417.7 4.5 %gather_fusion = f32[768]{0:T(1024)S(1)} fusion(f32[1536]{0:T(1024)S(1)} %reshape.115, s32[1024]{0:T(1024)S(1)} %pad_clamp_fusion), kind=kCustom, calls=%fused_computation | custom fusion | bytes 9216 | tf_op jit(solution)/shard_map/gather | solution.py:93
  422.2 3.9 scatter_custom_fusion.2
  (61 shorter events, 0.4 us)
Async XLA Ops:
  8.0 5.3 %copy-start = (f32[768,768]{1,0:T(8,128)S(1)}, f32[768,768]{1,0:T(8,128)}, u32[]{:S(2)}) copy-start(f32[768,768]{1,0:T(8,128)} %param.6) | copy-start | bytes 7077892
  23.1 9.7 %copy-start.2 = (s32[512]{0:T(512)S(1)}, s32[512]{0:T(512)}, u32[]{:S(2)}) copy-start(s32[512]{0:T(512)} %param.8) | copy-start | bytes 6148
  23.1 10.1 %copy-start.3 = (s32[768]{0:T(1024)S(1)}, s32[768]{0:T(1024)}, u32[]{:S(2)}) copy-start(s32[768]{0:T(1024)} %param.7) | copy-start | bytes 9220
  23.1 69.2 %all-to-all-start.1 = ((f32[32,48,768]{2,1,0:T(8,128)}), f32[32,48,768]{2,1,0:T(8,128)}, u32[]{:S(2)}, u32[]{:S(2)}) async-start(f32[32,48,768]{2,1,0:T(8,128)} %bitcast.46), calls=%async_computation.1 | async-start | bytes 9437184 | tf_op jit(solution)/shard_map/all_to_all | solution.py:71
  32.7 92.4 %reduce-scatter.2.cloned.1.call-start = ((), (), s32[]{:S(2)}) async-start(), calls=%async_computation.5 | async-start | bytes 1622016 | tf_op jit(solution)/shard_map/reduce_scatter | solution.py:108
  37.0 232.4 %all-gather.3.cloned.1.call-start = ((), (), s32[]{:S(2)}) async-start(), calls=%async_computation.4 | async-start | bytes 23592960 | tf_op jit(solution)/shard_map/all_gather | solution.py:87
  92.3 13.9 %copy-start.4 = (s32[768]{0:T(1024)S(1)}, s32[768]{0:T(1024)}, u32[]{:S(2)}) copy-start(s32[768]{0:T(1024)} %param.9) | copy-start | bytes 9220
  96.4 16.6 %all-to-all-start = ((s32[32,1,48]{2,1,0:T(1,128)}), s32[32,1,48]{2,1,0:T(1,128)S(1)}, u32[]{:S(2)}, u32[]{:S(2)}) async-start(s32[32,1,48]{2,1,0:T(1,128)} %all_to_all.17), calls=%async_computation | async-start | bytes 32768 | tf_op jit(solution)/shard_map/all_to_all | solution.py:78
  113.1 156.3 %copy-start.1 = (s32[32,1,48]{2,1,0:T(1,128)}, s32[32,1,48]{2,1,0:T(1,128)S(1)}, u32[]{:S(2)}) copy-start(s32[32,1,48]{2,1,0:T(1,128)S(1)} %all-to-all-done) | copy-start | bytes 18436
  401.7 14.7 %all-to-all-start.2 = ((f32[32,1,48]{2,1,0:T(1,128)}), f32[32,1,48]{2,1,0:T(1,128)S(1)}, u32[]{:S(2)}, u32[]{:S(2)}) async-start(f32[32,1,48]{2,1,0:T(1,128)} %all_to_all.21), calls=%async_computation.2 | async-start | bytes 32768 | tf_op jit(solution)/shard_map/all_to_all | solution.py:90
Sparse Core Ops, SparseCore 0:
  37.1 80.2 reduce-scatter.1
Sparse Core Ops, SparseCore 1:
  92.4 176.9 all-gather.2
where the time goes:
time: 434 us
  waiting for transfers between devices  196 us (45%)
  matrix products  135 us (31%)
  starting transfers between devices  27.2 us (6%)
  blocking collectives  27 us (6%)
  other arithmetic  17.5 us (4%)
  between operations  15.7 us (4%)
  local copies, waits for them, and re-layouts  14.8 us (3%)
    dot_general x12, matrix products, masked_weights(): jnp.einsum('id,jd->ij', left_rows, right_rows, preferred_element_type=jnp...  131 us
    all_gather x1, waiting for transfers between devices, local(): lax.all_gather(held_rows, 'grp', axis=0, tiled=True)  128 us
    all_to_all x1, waiting for transfers between devices, local(): lax.all_to_all(send_rows.reshape(owner_count, capacity, feature_width), '...  55.2 us
    psum x1, blocking collectives, local(): cluster_sums = lax.psum(partial_value, 'grp')  16.3 us
    all_gather x1, blocking collectives, local(): lax.all_gather(held_ids, 'grp', axis=0, tiled=True)  10.7 us
    all_to_all x1, starting transfers between devices, local(): lax.all_to_all(send_ids.reshape(owner_count, capacity), 'own', split_axis...  9.77 us
    scatter x1, other arithmetic, local(): jnp.zeros((slot_count, feature_width), jnp.float32).at[slot_index]  9.72 us
    all_to_all x1, starting transfers between devices, local(): lax.all_to_all(send_rows.reshape(owner_count, capacity, feature_width), '...  9.61 us
  transfers between devices with their start and end apart: 5, of which 4 were waited for; matrix products, arithmetic and copies ran while one was open for 2% of the time, Pallas kernels for 0%

commit v1 on v0

--- a/solution.py
+++ b/solution.py
@@ -106,7 +106,7 @@
         precision=lax.Precision.HIGHEST,
     )
     partial_value = lax.psum_scatter(cluster_terms, "own", scatter_dimension=0, tiled=True)
-    cluster_sums = lax.psum(partial_value, "grp")
+    cluster_sums = jnp.sum(lax.all_gather(partial_value, "grp"), axis=0)
     centroids = cluster_sums * lax.rsqrt(
         jnp.mean(cluster_sums * cluster_sums, axis=1, keepdims=True) + 1e-06
     )

time: 434 us -> 435 us (level)
  waiting for transfers between devices: 196 us -> 202 us
  blocking collectives: 27 us -> 22.2 us
    psum x1 -> x0, blocking collectives: 16.3 us -> none  [local(): cluster_sums = lax.psum(partial_value, 'grp')]
    all_gather x0 -> x1, blocking collectives: none -> 11.5 us  [local(): cluster_sums = jnp.sum(lax.all_gather(partial_value, 'grp'), axis=0)]
    all_gather x1, waiting for transfers between devices: 128 us -> 133 us  [local(): lax.all_gather(held_rows, 'grp', axis=0, tiled=True)]
where the time goes in v1:
time: 435 us; the launch traced here: 434 us
  waiting for transfers between devices  202 us (46%)
  matrix products  135 us (31%)
  starting transfers between devices  27.2 us (6%)
  blocking collectives  22.2 us (5%)
  other arithmetic  17.5 us (4%)
  between operations  15.7 us (4%)
  local copies, waits for them, and re-layouts  14.8 us (3%)
    all_gather x1, waiting for transfers between devices, local(): lax.all_gather(held_rows, 'grp', axis=0, tiled=True)  133 us
    dot_general x12, matrix products, masked_weights(): jnp.einsum('id,jd->ij', left_rows, right_rows, preferred_element_type=jnp...  131 us
    all_to_all x1, waiting for transfers between devices, local(): lax.all_to_all(send_rows.reshape(owner_count, capacity, feature_width), '...  55.2 us
    all_gather x1, blocking collectives, local(): cluster_sums = jnp.sum(lax.all_gather(partial_value, 'grp'), axis=0)  11.5 us
    all_gather x1, blocking collectives, local(): lax.all_gather(held_ids, 'grp', axis=0, tiled=True)  10.7 us
    all_to_all x1, starting transfers between devices, local(): lax.all_to_all(send_ids.reshape(owner_count, capacity), 'own', split_axis...  9.77 us
    scatter x1, other arithmetic, local(): jnp.zeros((slot_count, feature_width), jnp.float32).at[slot_index]  9.72 us
    all_to_all x1, starting transfers between devices, local(): lax.all_to_all(send_rows.reshape(owner_count, capacity, feature_width), '...  9.61 us
  transfers between devices with their start and end apart: 5, of which 4 were waited for; matrix products, arithmetic and copies ran while one was open for 2% of the time, Pallas kernels for 0%

profile of v1, /device:TPU:1, one launch (start us, length us, event | category | flops | bytes accessed | tf_op | source)
XLA Modules:
  0.0 434.2 jit_solution(9705970876401286471)
XLA Ops:
  8.0 1.2 select_reduce_fusion
  9.2 1.7 reduce-window.6
  11.0 0.3 slice_reduce_fusion
  11.3 0.1 fusion.22
  11.4 1.9 multiply_reduce_fusion
  13.3 9.7 %scatter_custom_fusion.1 = f32[1536,768]{1,0:T(8,128)} fusion(s32[768]{0:T(1024)S(1)} %fusion.26, f32[]{:T(128)} %constant.55.clone.1, f32[768,768]{1,0:T(8,128)S(1)} %copy-done, f32[768]{0:T(1024)S(1)} %add_rsqrt_fusion), kind=kCustom, calls=%fused_computation.17 | custom fusion | flops 589824 | bytes 7081988 | tf_op jit(solution)/shard_map/scatter | solution.py:68
  23.1 9.6 %all-to-all-start.1 = ((f32[32,48,768]{2,1,0:T(8,128)}), f32[32,48,768]{2,1,0:T(8,128)}, u32[]{:S(2)}, u32[]{:S(2)}) async-start(f32[32,48,768]{2,1,0:T(8,128)} %bitcast.47), calls=%async_computation.1 | async-start | bytes 9437184 | tf_op jit(solution)/shard_map/all_to_all | solution.py:71
  32.7 0.0 reduce-scatter.2.cloned.1.call-start
  32.8 0.2 convert_reduce_fusion
  33.0 0.2 select_reduce_fusion.1
  33.2 3.8 fusion.12
  37.0 0.0 all-gather.4.cloned.1.call-start
  37.1 55.2 %all-to-all-done.1 = f32[32,48,768]{2,1,0:T(8,128)} async-done(((f32[32,48,768]{2,1,0:T(8,128)}), f32[32,48,768]{2,1,0:T(8,128)}, u32[]{:S(2)}, u32[]{:S(2)}) %all-to-all-start.1) | async-done | bytes 4718624 | tf_op jit(solution)/shard_map/all_to_all | solution.py:71
  92.3 3.4 scatter_custom_fusion
  95.7 0.7 all_to_all.17
  96.4 9.8 %all-to-all-start = ((s32[32,1,48]{2,1,0:T(1,128)}), s32[32,1,48]{2,1,0:T(1,128)S(1)}, u32[]{:S(2)}, u32[]{:S(2)}) async-start(s32[32,1,48]{2,1,0:T(1,128)} %all_to_all.17), calls=%async_computation | async-start | bytes 32768 | tf_op jit(solution)/shard_map/all_to_all | solution.py:78
  106.2 6.8 %all-to-all-done = s32[32,1,48]{2,1,0:T(1,128)S(1)} async-done(((s32[32,1,48]{2,1,0:T(1,128)}), s32[32,1,48]{2,1,0:T(1,128)S(1)}, u32[]{:S(2)}, u32[]{:S(2)}) %all-to-all-start) | async-done | bytes 6176 | tf_op jit(solution)/shard_map/all_to_all | solution.py:78
  113.1 0.1 eq.172
  113.1 0.5 broadcast.158
  113.7 0.6 reduce.11
  114.3 0.1 reshape.150
  114.4 10.7 %all-gather.1 = s32[4,1,1536]{2,1,0:T(1,128)S(1)} all-gather(s32[1,1,1536]{2,1,0:T(1,128)S(1)} %reshape.150), channel_id=1, replica_groups=mesh['grp'=4,'own'=32] {'grp'}, dimensions={0}, use_global_device_ids=true | all-gather | bytes 30720 | tf_op jit(solution)/shard_map/all_gather | solution.py:88
  125.0 0.1 reduce.3
  125.1 11.5 %all-gather = f32[64,768]{1,0:T(8,128)S(1)} all-gather(f32[16,768]{1,0:T(8,128)} %reduce-scatter.2.cloned.1.call-done), channel_id=2, replica_groups=mesh['grp'=4,'own'=32] {'grp'}, dimensions={0}, use_global_device_ids=true | all-gather | bytes 245760 | tf_op jit(solution)/shard_map/all_gather | solution.py:109
  136.7 0.1 multiply_reduce_fusion.1
  136.8 133.2 %all-gather.4.cloned.1.call-done = f32[6144,768]{1,0:T(8,128)} async-done(((f32[1536,768]{1,0:T(8,128)}), f32[6144,768]{1,0:T(8,128)}) %all-gather.4.cloned.1.call-update) | async-done | bytes 18874384 | tf_op jit(solution)/shard_map/all_gather | solution.py:87
  270.0 131.6 %while.14 = (s32[]{:T(128)}, f32[1536]{0:T(1024)S(1)}, s32[32,48]{1,0:T(8,128)}, s32[12,512]{1,0:T(8,128)S(1)}, f32[12,512,768]{2,1,0:T(8,128)}, /*index=5*/f32[...) while((s32[]{:T(128)}, f32[1536]{0:T(1024)S(1)}, s32[32,48]{1,0:T(8,128)}, ...), condition=%wide.wide.region_9.10_spmd.clone, body=%wide.wide.region_7.9_spmd.clone.sunk | while | flops 7252478976 | bytes 6338155 | solution.py:47
  270.0 10.9 %fusion.38 = f32[1536]{0:T(1024)S(1)} fusion(f32[1536,768]{1,0:T(8,128)} %get-tuple-element.203, f32[12,512,768]{2,1,0:T(8,128)} %get-tuple-element.202, s32[]{:T(128)} %get-tuple-element.189, pred[1536]{0:T(1024)(128)(4,1)S(1)} %broadcast_compare_fusion.3, s32[512]{0:T(512)S(1)} %bitcast.52, s32[1536]{0:T(1024)S(1)} %get-tuple-element.204), kind=kOutput, calls=%fused_computation.11.clone.clone.1 | convolution fusion | flops 7252474368 | bytes 6307840 | tf_op jit(solution)/shard_map/while/body/eval_jaxpr/id,jd->ij/dot_general | solution.py:24
  281.0 10.9 %fusion.38 = f32[1536]{0:T(1024)S(1)} fusion(f32[1536,768]{1,0:T(8,128)} %get-tuple-element.203, f32[12,512,768]{2,1,0:T(8,128)} %get-tuple-element.202, s32[]{:T(128)} %get-tuple-element.189, pred[1536]{0:T(1024)(128)(4,1)S(1)} %broadcast_compare_fusion.3, s32[512]{0:T(512)S(1)} %bitcast.52, s32[1536]{0:T(1024)S(1)} %get-tuple-element.204), kind=kOutput, calls=%fused_computation.11.clone.clone.1 | convolution fusion | flops 7252474368 | bytes 6307840 | tf_op jit(solution)/shard_map/while/body/eval_jaxpr/id,jd->ij/dot_general | solution.py:24
  292.0 10.9 %fusion.38 = f32[1536]{0:T(1024)S(1)} fusion(f32[1536,768]{1,0:T(8,128)} %get-tuple-element.203, f32[12,512,768]{2,1,0:T(8,128)} %get-tuple-element.202, s32[]{:T(128)} %get-tuple-element.189, pred[1536]{0:T(1024)(128)(4,1)S(1)} %broadcast_compare_fusion.3, s32[512]{0:T(512)S(1)} %bitcast.52, s32[1536]{0:T(1024)S(1)} %get-tuple-element.204), kind=kOutput, calls=%fused_computation.11.clone.clone.1 | convolution fusion | flops 7252474368 | bytes 6307840 | tf_op jit(solution)/shard_map/while/body/eval_jaxpr/id,jd->ij/dot_general | solution.py:24
  303.0 10.9 %fusion.38 = f32[1536]{0:T(1024)S(1)} fusion(f32[1536,768]{1,0:T(8,128)} %get-tuple-element.203, f32[12,512,768]{2,1,0:T(8,128)} %get-tuple-element.202, s32[]{:T(128)} %get-tuple-element.189, pred[1536]{0:T(1024)(128)(4,1)S(1)} %broadcast_compare_fusion.3, s32[512]{0:T(512)S(1)} %bitcast.52, s32[1536]{0:T(1024)S(1)} %get-tuple-element.204), kind=kOutput, calls=%fused_computation.11.clone.clone.1 | convolution fusion | flops 7252474368 | bytes 6307840 | tf_op jit(solution)/shard_map/while/body/eval_jaxpr/id,jd->ij/dot_general | solution.py:24
  313.9 10.9 %fusion.38 = f32[1536]{0:T(1024)S(1)} fusion(f32[1536,768]{1,0:T(8,128)} %get-tuple-element.203, f32[12,512,768]{2,1,0:T(8,128)} %get-tuple-element.202, s32[]{:T(128)} %get-tuple-element.189, pred[1536]{0:T(1024)(128)(4,1)S(1)} %broadcast_compare_fusion.3, s32[512]{0:T(512)S(1)} %bitcast.52, s32[1536]{0:T(1024)S(1)} %get-tuple-element.204), kind=kOutput, calls=%fused_computation.11.clone.clone.1 | convolution fusion | flops 7252474368 | bytes 6307840 | tf_op jit(solution)/shard_map/while/body/eval_jaxpr/id,jd->ij/dot_general | solution.py:24
  324.9 10.9 %fusion.38 = f32[1536]{0:T(1024)S(1)} fusion(f32[1536,768]{1,0:T(8,128)} %get-tuple-element.203, f32[12,512,768]{2,1,0:T(8,128)} %get-tuple-element.202, s32[]{:T(128)} %get-tuple-element.189, pred[1536]{0:T(1024)(128)(4,1)S(1)} %broadcast_compare_fusion.3, s32[512]{0:T(512)S(1)} %bitcast.52, s32[1536]{0:T(1024)S(1)} %get-tuple-element.204), kind=kOutput, calls=%fused_computation.11.clone.clone.1 | convolution fusion | flops 7252474368 | bytes 6307840 | tf_op jit(solution)/shard_map/while/body/eval_jaxpr/id,jd->ij/dot_general | solution.py:24
  335.9 10.9 %fusion.38 = f32[1536]{0:T(1024)S(1)} fusion(f32[1536,768]{1,0:T(8,128)} %get-tuple-element.203, f32[12,512,768]{2,1,0:T(8,128)} %get-tuple-element.202, s32[]{:T(128)} %get-tuple-element.189, pred[1536]{0:T(1024)(128)(4,1)S(1)} %broadcast_compare_fusion.3, s32[512]{0:T(512)S(1)} %bitcast.52, s32[1536]{0:T(1024)S(1)} %get-tuple-element.204), kind=kOutput, calls=%fused_computation.11.clone.clone.1 | convolution fusion | flops 7252474368 | bytes 6307840 | tf_op jit(solution)/shard_map/while/body/eval_jaxpr/id,jd->ij/dot_general | solution.py:24
  346.8 10.9 %fusion.38 = f32[1536]{0:T(1024)S(1)} fusion(f32[1536,768]{1,0:T(8,128)} %get-tuple-element.203, f32[12,512,768]{2,1,0:T(8,128)} %get-tuple-element.202, s32[]{:T(128)} %get-tuple-element.189, pred[1536]{0:T(1024)(128)(4,1)S(1)} %broadcast_compare_fusion.3, s32[512]{0:T(512)S(1)} %bitcast.52, s32[1536]{0:T(1024)S(1)} %get-tuple-element.204), kind=kOutput, calls=%fused_computation.11.clone.clone.1 | convolution fusion | flops 7252474368 | bytes 6307840 | tf_op jit(solution)/shard_map/while/body/eval_jaxpr/id,jd->ij/dot_general | solution.py:24
  357.8 10.9 %fusion.38 = f32[1536]{0:T(1024)S(1)} fusion(f32[1536,768]{1,0:T(8,128)} %get-tuple-element.203, f32[12,512,768]{2,1,0:T(8,128)} %get-tuple-element.202, s32[]{:T(128)} %get-tuple-element.189, pred[1536]{0:T(1024)(128)(4,1)S(1)} %broadcast_compare_fusion.3, s32[512]{0:T(512)S(1)} %bitcast.52, s32[1536]{0:T(1024)S(1)} %get-tuple-element.204), kind=kOutput, calls=%fused_computation.11.clone.clone.1 | convolution fusion | flops 7252474368 | bytes 6307840 | tf_op jit(solution)/shard_map/while/body/eval_jaxpr/id,jd->ij/dot_general | solution.py:24
  368.8 10.9 %fusion.38 = f32[1536]{0:T(1024)S(1)} fusion(f32[1536,768]{1,0:T(8,128)} %get-tuple-element.203, f32[12,512,768]{2,1,0:T(8,128)} %get-tuple-element.202, s32[]{:T(128)} %get-tuple-element.189, pred[1536]{0:T(1024)(128)(4,1)S(1)} %broadcast_compare_fusion.3, s32[512]{0:T(512)S(1)} %bitcast.52, s32[1536]{0:T(1024)S(1)} %get-tuple-element.204), kind=kOutput, calls=%fused_computation.11.clone.clone.1 | convolution fusion | flops 7252474368 | bytes 6307840 | tf_op jit(solution)/shard_map/while/body/eval_jaxpr/id,jd->ij/dot_general | solution.py:24
  379.7 10.9 %fusion.38 = f32[1536]{0:T(1024)S(1)} fusion(f32[1536,768]{1,0:T(8,128)} %get-tuple-element.203, f32[12,512,768]{2,1,0:T(8,128)} %get-tuple-element.202, s32[]{:T(128)} %get-tuple-element.189, pred[1536]{0:T(1024)(128)(4,1)S(1)} %broadcast_compare_fusion.3, s32[512]{0:T(512)S(1)} %bitcast.52, s32[1536]{0:T(1024)S(1)} %get-tuple-element.204), kind=kOutput, calls=%fused_computation.11.clone.clone.1 | convolution fusion | flops 7252474368 | bytes 6307840 | tf_op jit(solution)/shard_map/while/body/eval_jaxpr/id,jd->ij/dot_general | solution.py:24
  390.7 10.9 %fusion.38 = f32[1536]{0:T(1024)S(1)} fusion(f32[1536,768]{1,0:T(8,128)} %get-tuple-element.203, f32[12,512,768]{2,1,0:T(8,128)} %get-tuple-element.202, s32[]{:T(128)} %get-tuple-element.189, pred[1536]{0:T(1024)(128)(4,1)S(1)} %broadcast_compare_fusion.3, s32[512]{0:T(512)S(1)} %bitcast.52, s32[1536]{0:T(1024)S(1)} %get-tuple-element.204), kind=kOutput, calls=%fused_computation.11.clone.clone.1 | convolution fusion | flops 7252474368 | bytes 6307840 | tf_op jit(solution)/shard_map/while/body/eval_jaxpr/id,jd->ij/dot_general | solution.py:24
  401.7 0.7 all_to_all.21
  402.3 7.7 %all-to-all-start.2 = ((f32[32,1,48]{2,1,0:T(1,128)}), f32[32,1,48]{2,1,0:T(1,128)S(1)}, u32[]{:S(2)}, u32[]{:S(2)}) async-start(f32[32,1,48]{2,1,0:T(1,128)} %all_to_all.21), calls=%async_computation.2 | async-start | bytes 32768 | tf_op jit(solution)/shard_map/all_to_all | solution.py:90
  410.1 0.7 broadcast_multiply_fusion
  410.8 6.2 %all-to-all-done.2 = f32[32,1,48]{2,1,0:T(1,128)S(1)} async-done(((f32[32,1,48]{2,1,0:T(1,128)}), f32[32,1,48]{2,1,0:T(1,128)S(1)}, u32[]{:S(2)}, u32[]{:S(2)}) %all-to-all-start.2) | async-done | bytes 6176 | tf_op jit(solution)/shard_map/all_to_all | solution.py:90
  417.0 0.5 broadcast.159
  417.5 0.7 reduce.12
  418.2 0.1 reshape.115
  418.3 4.5 %gather_fusion = f32[768]{0:T(1024)S(1)} fusion(f32[1536]{0:T(1024)S(1)} %reshape.115, s32[1024]{0:T(1024)S(1)} %pad_clamp_fusion), kind=kCustom, calls=%fused_computation | custom fusion | bytes 9216 | tf_op jit(solution)/shard_map/gather | solution.py:93
  422.8 3.9 scatter_custom_fusion.2
  (62 shorter events, 0.5 us)
Async XLA Ops:
  8.0 5.3 %copy-start = (f32[768,768]{1,0:T(8,128)S(1)}, f32[768,768]{1,0:T(8,128)}, u32[]{:S(2)}) copy-start(f32[768,768]{1,0:T(8,128)} %param.6) | copy-start | bytes 7077892
  23.1 9.7 %copy-start.2 = (s32[512]{0:T(512)S(1)}, s32[512]{0:T(512)}, u32[]{:S(2)}) copy-start(s32[512]{0:T(512)} %param.8) | copy-start | bytes 6148
  23.1 10.1 %copy-start.3 = (s32[768]{0:T(1024)S(1)}, s32[768]{0:T(1024)}, u32[]{:S(2)}) copy-start(s32[768]{0:T(1024)} %param.7) | copy-start | bytes 9220
  23.1 69.2 %all-to-all-start.1 = ((f32[32,48,768]{2,1,0:T(8,128)}), f32[32,48,768]{2,1,0:T(8,128)}, u32[]{:S(2)}, u32[]{:S(2)}) async-start(f32[32,48,768]{2,1,0:T(8,128)} %bitcast.47), calls=%async_computation.1 | async-start | bytes 9437184 | tf_op jit(solution)/shard_map/all_to_all | solution.py:71
  32.7 92.4 %reduce-scatter.2.cloned.1.call-start = ((), (), s32[]{:S(2)}) async-start(), calls=%async_computation.5 | async-start | bytes 1622016 | tf_op jit(solution)/shard_map/reduce_scatter | solution.py:108
  37.0 233.0 %all-gather.4.cloned.1.call-start = ((), (), s32[]{:S(2)}) async-start(), calls=%async_computation.4 | async-start | bytes 23592960 | tf_op jit(solution)/shard_map/all_gather | solution.py:87
  92.3 13.9 %copy-start.4 = (s32[768]{0:T(1024)S(1)}, s32[768]{0:T(1024)}, u32[]{:S(2)}) copy-start(s32[768]{0:T(1024)} %param.9) | copy-start | bytes 9220
  96.4 16.6 %all-to-all-start = ((s32[32,1,48]{2,1,0:T(1,128)}), s32[32,1,48]{2,1,0:T(1,128)S(1)}, u32[]{:S(2)}, u32[]{:S(2)}) async-start(s32[32,1,48]{2,1,0:T(1,128)} %all_to_all.17), calls=%async_computation | async-start | bytes 32768 | tf_op jit(solution)/shard_map/all_to_all | solution.py:78
  113.1 157.0 %copy-start.1 = (s32[32,1,48]{2,1,0:T(1,128)}, s32[32,1,48]{2,1,0:T(1,128)S(1)}, u32[]{:S(2)}) copy-start(s32[32,1,48]{2,1,0:T(1,128)S(1)} %all-to-all-done) | copy-start | bytes 18436
  402.3 14.7 %all-to-all-start.2 = ((f32[32,1,48]{2,1,0:T(1,128)}), f32[32,1,48]{2,1,0:T(1,128)S(1)}, u32[]{:S(2)}, u32[]{:S(2)}) async-start(f32[32,1,48]{2,1,0:T(1,128)} %all_to_all.21), calls=%async_computation.2 | async-start | bytes 32768 | tf_op jit(solution)/shard_map/all_to_all | solution.py:90
Sparse Core Ops, SparseCore 0:
  37.1 80.2 reduce-scatter.1
Sparse Core Ops, SparseCore 1:
  92.4 177.6 all-gather.3
